TPU v7x, 32 devices: a whole 2x2x4 slice. The times are simulated.
32 devices in a mesh: row: 4 (over y, core), col: 8 (over z, x).
Axes of the slice: x: 2, y: 2, z: 4, core: 2. Of those that a mesh axis runs over, the one named last changes fastest.
Arguments:
- inputs: bfloat16 [512, 8192], P('row', 'col'), may hold values from -6 to 6
- grad_out: bfloat16 [512, 8192], P('row', 'col'), may hold values from -1.5 to 1.5
- up_blocks: bfloat16 [8, 1024, 128], P('row', 'col'), may hold values from -0.5 to 0.5
- up_where: int32 [8, 16], P('row', 'col'), may hold values from -1 to 47, as said below
- down_blocks: bfloat16 [8, 1024, 128], P('row', 'col'), may hold values from -0.5 to 0.5
- down_where: int32 [8, 16], P('row', 'col'), may hold values from -1 to 47, as said below
Outputs:
- grad_in: bfloat16 [512, 8192], P('row', 'col')
- up_grad: bfloat16 [8, 1024, 128], P('row', 'col')
- down_grad: bfloat16 [8, 1024, 128], P('row', 'col')
Inputs may be any that keep to these rules, and one draw needn't show every extreme that they name: `up_where`: each grid owner (r, c) has 2 slots; a used slot names a block row below 16 and a block column below 48 of the owner's part of W1, used slots of one owner name distinct blocks and come first, unused slots hold -1 in both entries. In some grid column every owner uses all 2 slots, and some owner leaves a slot unused. `down_where`: as for up_where, with the first entry a hidden block below 48 and the second a model-width block below 16 of the owner's part of W2.
All inputs are finite; a program needn't handle non-finite values.
Results may differ from a plain program's by a relative error of at most 0.013.
Values may be sent and summed in bfloat16 or wider, within the bound.
A program may use at most 64 MiB of HBM per device.

v0:
```python
import jax
import jax.numpy as jnp
from jax import lax
from jax.sharding import PartitionSpec as P

FF = 49152


def gelu_parts(hidden):
    cube = hidden * hidden * hidden
    inner = 0.7978845608028654 * (hidden + 0.044715 * cube)
    tanh_val = jnp.tanh(inner)
    value = 0.5 * hidden * (1.0 + tanh_val)
    slope = 0.5 * (1.0 + tanh_val) + 0.5 * hidden * (
        1.0 - tanh_val * tanh_val
    ) * 0.7978845608028654 * (1.0 + 0.134145 * hidden * hidden)
    return (value, slope)


def body(inputs, grad_out, up_blocks, up_where, down_blocks, down_where):
    block_side = up_blocks.shape[1]
    slot_count = up_blocks.shape[0]
    tok_rows = inputs.shape[0]
    row_count = lax.axis_size("row")
    col_count = lax.axis_size("col")
    width = inputs.shape[1] * col_count
    d_count = width // block_side
    row_blocks = d_count // row_count
    col_blocks = FF // (block_side * col_count)
    up_mat, up_pos, down_mat, down_pos = (
        lax.all_gather(up_blocks, "row", axis=0, tiled=True),
        lax.all_gather(up_where, "row", axis=0, tiled=True),
        lax.all_gather(down_blocks, "row", axis=0, tiled=True),
        lax.all_gather(down_where, "row", axis=0, tiled=True),
    )
    all_slots = up_mat.shape[0]
    owner_idx = jnp.arange(all_slots, dtype=jnp.int32) // slot_count
    up_valid = up_pos[:, 1] >= 0
    up_row = jnp.where(up_valid, owner_idx * row_blocks + up_pos[:, 0], 0)
    up_col = jnp.where(up_valid, up_pos[:, 1], 0)
    up_mat = jnp.where(up_valid[:, None, None], up_mat, jnp.zeros_like(up_mat))
    down_valid = down_pos[:, 0] >= 0
    down_frow = jnp.where(down_valid, down_pos[:, 0], 0)
    down_dcol = jnp.where(down_valid, owner_idx * row_blocks + down_pos[:, 1], 0)
    down_mat = jnp.where(down_valid[:, None, None], down_mat, jnp.zeros_like(down_mat))
    whole_in, whole_grad = (
        lax.all_gather(inputs, "col", axis=1, tiled=True),
        lax.all_gather(grad_out, "col", axis=1, tiled=True),
    )
    x_sel = jnp.take(whole_in.reshape(tok_rows, d_count, block_side), up_row, axis=1)
    y_sel = jnp.take(whole_grad.reshape(tok_rows, d_count, block_side), down_dcol, axis=1)
    block_out = jnp.einsum("tsk,skj->tsj", x_sel, up_mat, preferred_element_type=jnp.float32)
    hidden = jnp.zeros((tok_rows, col_blocks, block_side), jnp.float32).at[:, up_col].add(block_out)
    value, slope = gelu_parts(hidden)
    act = value.astype(jnp.bfloat16)
    act_sel = jnp.take(act, down_frow, axis=1)
    down_terms = jnp.einsum("tsf,tsd->sfd", act_sel, y_sel, preferred_element_type=jnp.float32)
    down_terms = jnp.where(down_valid[:, None, None], down_terms, jnp.zeros_like(down_terms))
    down_grad = lax.psum_scatter(
        down_terms.astype(jnp.bfloat16), "row", scatter_dimension=0, tiled=True
    )
    down_part = jnp.einsum("tsd,sfd->tsf", y_sel, down_mat, preferred_element_type=jnp.float32)
    grad_act = (
        jnp.zeros((tok_rows, col_blocks, block_side), jnp.float32).at[:, down_frow].add(down_part)
    )
    grad_hidden = (grad_act * slope).astype(jnp.bfloat16)
    dh_sel = jnp.take(grad_hidden, up_col, axis=1)
    up_terms = jnp.einsum("tsk,tsj->skj", x_sel, dh_sel, preferred_element_type=jnp.float32)
    up_terms = jnp.where(up_valid[:, None, None], up_terms, jnp.zeros_like(up_terms))
    up_grad = lax.psum_scatter(
        up_terms.astype(jnp.bfloat16), "row", scatter_dimension=0, tiled=True
    )
    back = jnp.einsum("tsj,skj->tsk", dh_sel, up_mat, preferred_element_type=jnp.float32)
    partial_value = (
        jnp.zeros((tok_rows, d_count, block_side), jnp.float32)
        .at[:, up_row]
        .add(back)
        .reshape(tok_rows, width)
    )
    grad_in = lax.psum_scatter(
        partial_value.astype(jnp.bfloat16), "col", scatter_dimension=1, tiled=True
    )
    return (grad_in, up_grad, down_grad)


def solution(mesh):
    placed = (
        P("row", "col"),
        P("row", "col"),
        P("row", "col", None),
        P("row", "col"),
        P("row", "col", None),
        P("row", "col"),
    )
    return jax.shard_map(
        body,
        mesh=mesh,
        in_specs=placed,
        out_specs=(P("row", "col"), P("row", "col", None), P("row", "col", None)),
        check_vma=False,
    )
```

profile of v0, /device:TPU:0, one launch (start us, length us, event | category | flops | bytes accessed | tf_op | source)
XLA Modules:
  0.0 267.0 jit_solution(7735589844905739753)
XLA Ops:
  7.2 0.0 all-gather.7.cloned.1.call-start
  7.2 1.8 copy.33
  9.0 0.0 all-gather.7.cloned.1.call-update
  9.0 0.0 all-gather.5.cloned.1.call-start
  9.1 1.8 copy.31
  10.9 0.0 all-gather.5.cloned.1.call-update
  10.9 0.0 reduce-scatter.4.cloned.1.call-start
  10.9 6.3 %all-gather = s32[4,2,2]{2,1,0:T(2,128)S(1)} all-gather(s32[1,2,2]{2,1,0:T(2,128)} %bitcast.72), channel_id=1, replica_groups=mesh['row'=4,'col'=8] {'row'}, dimensions={0}, use_global_device_ids=true | all-gather | bytes 80 | tf_op jit(solution)/shard_map/all_gather | solution.py:32
  17.3 5.5 %all-gather.1 = s32[4,2,2]{2,1,0:T(2,128)S(1)} all-gather(s32[1,2,2]{2,1,0:T(2,128)} %bitcast.73), channel_id=1, replica_groups=mesh['row'=4,'col'=8] {'row'}, dimensions={0}, use_global_device_ids=true | all-gather | bytes 80 | tf_op jit(solution)/shard_map/all_gather | solution.py:34
  22.8 0.1 fusion.43
  22.8 0.1 copy.46
  22.9 0.1 copy.45
  23.0 0.1 fusion.44
  23.1 0.1 copy.43
  23.2 0.1 copy.44
  23.2 6.2 %all_gather.19 = bf16[8,128,128]{2,1,0:T(8,128)(2,1)S(1)} all-gather(bf16[2,128,128]{2,1,0:T(8,128)(2,1)} %param.12), channel_id=1, replica_groups=mesh['row'=4,'col'=8] {'row'}, dimensions={0}, use_global_device_ids=true | all-gather | bytes 327680 | tf_op jit(solution)/shard_map/all_gather | solution.py:31
  29.4 7.8 %all_gather.21 = bf16[8,128,128]{2,1,0:T(8,128)(2,1)} all-gather(bf16[2,128,128]{2,1,0:T(8,128)(2,1)} %param.14), channel_id=1, replica_groups=mesh['row'=4,'col'=8] {'row'}, dimensions={0}, use_global_device_ids=true | all-gather | bytes 327680 | tf_op jit(solution)/shard_map/all_gather | solution.py:33
  37.3 25.2 %all-gather.7.cloned.1.call-done = bf16[128,8192]{0,1:T(8,128)(2,1)} async-done(((bf16[128,1024]{0,1:T(8,128)(2,1)}), bf16[128,8192]{0,1:T(8,128)(2,1)}) %all-gather.7.cloned.1.call-update) | async-done | bytes 2097168 | tf_op jit(solution)/shard_map/all_gather | solution.py:47
  62.5 3.2 %copy.34 = bf16[128,64,128]{2,0,1:T(8,128)(2,1)S(1)} copy(bf16[128,64,128]{0,2,1:T(8,128)(2,1)} %bitcast.68) | data formatting | bytes 4194304 | tf_op jit(solution)/shard_map/reshape | solution.py:50
  65.7 46.6 %all-gather.5.cloned.1.call-done = bf16[128,8192]{0,1:T(8,128)(2,1)} async-done(((bf16[128,1024]{0,1:T(8,128)(2,1)}), bf16[128,8192]{0,1:T(8,128)(2,1)}) %all-gather.5.cloned.1.call-update) | async-done | bytes 2097168 | tf_op jit(solution)/shard_map/all_gather | solution.py:48
  112.3 4.1 %copy.32 = bf16[128,64,128]{2,0,1:T(8,128)(2,1)} copy(bf16[128,64,128]{0,2,1:T(8,128)(2,1)} %bitcast.69) | data formatting | bytes 4194304 | tf_op jit(solution)/shard_map/reshape | solution.py:51
  116.4 0.6 gather_fusion.1
  117.0 0.0 copy-start
  117.0 3.0 %gather_fusion = bf16[8,128,128]{2,1,0:T(8,128)(2,1)} fusion(bf16[128,64,128]{2,0,1:T(8,128)(2,1)} %copy.32, s32[1024]{0:T(1024)S(1)} %pad_clamp_fusion.3), kind=kCustom, calls=%fused_computation.clone | custom fusion | bytes 524320 | tf_op jit(solution)/shard_map/jit(_take)/gather | solution.py:51
  119.9 1.1 fusion.16
  121.0 0.0 copy-done
  121.0 0.4 broadcast.142.clone
  121.4 2.0 scatter_fusion.1
  123.4 2.2 fusion.19
  125.6 2.0 broadcast.142.clone.1
  127.7 2.9 %scatter_fusion = f32[128,48,128]{2,0,1:T(8,128)} fusion(f32[128,48,128]{2,0,1:T(8,128)} %broadcast.142.clone.1, s32[8]{0:T(128)S(1)} %fusion.31, f32[8,128,128]{2,1,0:T(8,128)} %fusion.19), kind=kCustom, calls=%fused_computation.4 | custom fusion | flops 131072 | bytes 1572896 | tf_op jit(solution)/shard_map/scatter-add | solution.py:64
  130.6 4.8 %multiply_convert_fusion = (bf16[128,48,128]{2,0,1:T(8,128)(2,1)}, bf16[128,48,128]{2,0,1:T(8,128)(2,1)}) fusion(f32[128,48,128]{2,0,1:T(8,128)S(1)} %scatter_fusion.1, f32[128,48,128]{2,0,1:T(8,128)} %scatter_fusion), kind=kLoop, calls=%fused_computation.18 | loop fusion | flops 16515072 | bytes 9437184 | tf_op jit(solution)/shard_map/convert_element_type | solution.py:55
  135.4 2.0 gather_fusion.2
  137.4 0.4 fusion.13
  137.8 2.5 broadcast_in_dim.55
  140.3 2.7 %scatter_fusion.2 = f32[128,64,128]{2,0,1:T(8,128)} fusion(f32[128,64,128]{2,0,1:T(8,128)} %broadcast_in_dim.55, s32[8]{0:T(128)S(1)} %get-tuple-element.35, f32[8,128,128]{2,1,0:T(8,128)S(1)} %fusion.13), kind=kCustom, calls=%fused_computation.6 | custom fusion | flops 131072 | bytes 1572896 | tf_op jit(solution)/shard_map/scatter-add | solution.py:77
  143.0 2.6 convert_element_type.19
  145.6 0.0 copy-start.2
  145.6 0.0 copy-start.1
  145.6 2.9 %copy.35 = bf16[128,64,128]{0,2,1:T(8,128)(2,1)} copy(bf16[128,64,128]{2,0,1:T(8,128)(2,1)S(1)} %convert_element_type.19) | data formatting | bytes 4194304 | tf_op jit(solution)/shard_map/convert_element_type | solution.py:81
  148.5 0.0 reduce-scatter.4.cloned.1.call-update
  148.5 0.0 reduce-scatter.8.cloned.1.call-start
  148.6 2.0 gather_fusion.3
  150.6 0.0 copy-done.2
  150.6 1.1 fusion.10
  151.7 0.0 reduce-scatter.8.cloned.1.call-update
  151.7 0.0 reduce-scatter.6.cloned.1.call-start
  151.8 0.0 copy-done.1
  151.8 1.1 fusion.9
  152.8 0.0 reduce-scatter.6.cloned.1.call-update
  152.9 62.6 %reduce-scatter.4.cloned.1.call-done = bf16[128,1024]{0,1:T(8,128)(2,1)} async-done(((bf16[128,8192]{0,1:T(8,128)(2,1)}), bf16[128,1024]{0,1:T(8,128)(2,1)}) %reduce-scatter.4.cloned.1.call-update) | async-done | bytes 262160 | tf_op jit(solution)/shard_map/reduce_scatter | solution.py:80
  215.5 1.8 copy.38
  217.3 20.2 %reduce-scatter.8.cloned.1.call-done = bf16[2,128,128]{2,1,0:T(8,128)(2,1)} async-done(((bf16[8,128,128]{2,1,0:T(8,128)(2,1)}), bf16[2,128,128]{2,1,0:T(8,128)(2,1)}) %reduce-scatter.8.cloned.1.call-update) | async-done | bytes 65552 | tf_op jit(solution)/shard_map/reduce_scatter | solution.py:59
  237.5 23.0 %reduce-scatter.6.cloned.1.call-done = bf16[2,128,128]{2,1,0:T(8,128)(2,1)} async-done(((bf16[8,128,128]{2,1,0:T(8,128)(2,1)}), bf16[2,128,128]{2,1,0:T(8,128)(2,1)}) %reduce-scatter.6.cloned.1.call-update) | async-done | bytes 65552 | tf_op jit(solution)/shard_map/reduce_scatter | solution.py:70
  (7 shorter events, 0.1 us)
Async XLA Ops:
  7.2 55.3 %all-gather.7.cloned.1.call-start = ((), (), s32[]{:S(2)}) async-start(), calls=%async_computation.4 | async-start | bytes 2359296 | tf_op jit(solution)/shard_map/all_gather | solution.py:47
  9.0 103.3 %all-gather.5.cloned.1.call-start = ((), (), s32[]{:S(2)}) async-start(), calls=%async_computation.3 | async-start | bytes 2359296 | tf_op jit(solution)/shard_map/all_gather | solution.py:48
  10.9 204.6 %reduce-scatter.4.cloned.1.call-start = ((), (), s32[]{:S(2)}) async-start(), calls=%async_computation.5 | async-start | bytes 2359296 | tf_op jit(solution)/shard_map/reduce_scatter | solution.py:80
  117.0 4.1 %copy-start = (bf16[8,128,128]{2,1,0:T(8,128)(2,1)}, bf16[8,128,128]{2,1,0:T(8,128)(2,1)S(1)}, u32[]{:S(2)}) copy-start(bf16[8,128,128]{2,1,0:T(8,128)(2,1)S(1)} %gather_fusion.1) | copy-start | bytes 786436
  145.6 5.0 %copy-start.2 = (bf16[8,128,128]{2,1,0:T(8,128)(2,1)S(1)}, bf16[8,128,128]{2,1,0:T(8,128)(2,1)}, u32[]{:S(2)}) copy-start(bf16[8,128,128]{2,1,0:T(8,128)(2,1)} %gather_fusion) | copy-start | bytes 786436
  145.6 6.2 %copy-start.1 = (bf16[8,128,128]{2,1,0:T(8,128)(2,1)S(1)}, bf16[8,128,128]{2,1,0:T(8,128)(2,1)}, u32[]{:S(2)}) copy-start(bf16[8,128,128]{2,1,0:T(8,128)(2,1)} %copy-done) | copy-start | bytes 786436
  148.5 89.0 %reduce-scatter.8.cloned.1.call-start = ((), (), s32[]{:S(2)}) async-start(), calls=%async_computation.7 | async-start | bytes 327680 | tf_op jit(solution)/shard_map/reduce_scatter | solution.py:59
  151.7 108.8 %reduce-scatter.6.cloned.1.call-start = ((), (), s32[]{:S(2)}) async-start(), calls=%async_computation.6 | async-start | bytes 327680 | tf_op jit(solution)/shard_map/reduce_scatter | solution.py:70
Sparse Core Ops, SparseCore 0:
  10.7 51.7 all-gather.6
  64.6 47.6 all-gather.4
  148.6 66.7 reduce-scatter.3
  218.4 19.1 reduce-scatter.7
  240.4 20.0 reduce-scatter.5
where the time goes:
time: 268 us; the launch traced here: 267 us
  waiting for transfers between devices  178 us (66%)
  local copies, waits for them, and re-layouts  28.5 us (11%)
  blocking collectives  25.8 us (10%)
  other arithmetic  15.1 us (6%)
  between operations  13.9 us (5%)
  matrix products  5.79 us (2%)
    reduce_scatter x1, waiting for transfers between devices, body(): lax.psum_scatter(partial_value.astype(jnp.bfloat16), 'col', scatter_dimen...  62.6 us
    all_gather x1, waiting for transfers between devices, body(): lax.all_gather(grad_out, 'col', axis=1, tiled=True)  46.6 us
    all_gather x1, waiting for transfers between devices, body(): lax.all_gather(inputs, 'col', axis=1, tiled=True)  25.2 us
    reduce_scatter x1, waiting for transfers between devices, body(): lax.psum_scatter(up_terms.astype(jnp.bfloat16), 'row', scatter_dimension=...  23 us
    reduce_scatter x1, waiting for transfers between devices, body(): lax.psum_scatter(down_terms.astype(jnp.bfloat16), 'row', scatter_dimensio...  20.2 us
    all_gather x1, blocking collectives, body(): lax.all_gather(down_blocks, 'row', axis=0, tiled=True)  7.8 us
    all_gather x1, blocking collectives, body(): lax.all_gather(up_where, 'row', axis=0, tiled=True)  6.32 us
    all_gather x1, blocking collectives, body(): lax.all_gather(up_blocks, 'row', axis=0, tiled=True)  6.15 us
  transfers between devices with their start and end apart: 5, of which 5 were waited for; matrix products, arithmetic and copies ran while one was open for 4% of the time, Pallas kernels for 0%

commit v1 on v0

v1 whole, which is shorter than its diff:
```python
import functools

import jax
import jax.numpy as jnp
from jax import lax
from jax.experimental import pallas as pl
from jax.experimental.pallas import tpu as pltpu
from jax.sharding import PartitionSpec as P

MESH = pl.DeviceIdType.MESH
CHUNKS = 2


def gelu_parts(hidden):
    cube = hidden * hidden * hidden
    inner = 0.7978845608028654 * (hidden + 0.044715 * cube)
    tanh_val = jnp.tanh(inner)
    value = 0.5 * hidden * (1.0 + tanh_val)
    slope = 0.5 * (1.0 + tanh_val) + 0.5 * hidden * (
        1.0 - tanh_val * tanh_val
    ) * 0.7978845608028654 * (1.0 + 0.134145 * hidden * hidden)
    return (value, slope)


def dot(left, right, left_dim, right_dim):
    return lax.dot_general(
        left, right, (((left_dim,), (right_dim,)), ((), ())),
        preferred_element_type=jnp.float32,
    )


def flag(pred):
    return pred.astype(jnp.float32)


def kernel(
    rows, pairs, slots, chunks,
    x_hbm, y_hbm, up_hbm, dn_hbm, up_pos, dn_pos,
    gin_ref, ugrad_ref, dgrad_ref,
    own_pos, row_pos, grp_pos, row_tab, grp_tab,
    x_all, y_all, x_out, y_out, x_sel, y_sel,
    up_mat, dn_mat, block_out, down_part, act, dhid,
    back_out, back_in, fold_out, fold_in,
    up_out, up_in, dn_out, dn_in,
    loc_sem, own_sem, tab_sem,
    rp_send, rp_recv, gp_send, gp_recv, ex_send, ex_recv, w_send, w_recv,
    sel_send, sel_recv, bk_send, bk_recv, fx_send, fx_recv, gr_send, gr_recv,
):
    row = lax.axis_index("row")
    col = lax.axis_index("col")
    group, part = col // pairs, col % pairs
    tok = x_hbm.shape[0]
    blk = up_hbm.shape[1]
    wide = x_hbm.shape[1] // blk
    step = tok // chunks
    total = rows * slots

    def row_peer(k):
        return (lax.rem(row + k, rows), col)

    def grp_of(k):
        return lax.rem(group + k, rows)

    def grp_peer(k):
        return (row, grp_of(k) * pairs + part)

    def part_of(k):
        return lax.rem(part + k, pairs)

    def part_peer(k):
        return (row, group * pairs + part_of(k))

    def remote(src, dst, send, recv, peer):
        return pltpu.make_async_remote_copy(
            src_ref=src, dst_ref=dst, send_sem=send, recv_sem=recv,
            device_id=peer, device_id_type=MESH,
        )

    peers = [row_peer(k) for k in range(1, rows)]
    peers += [grp_peer(k) for k in range(1, rows)]
    peers += [part_peer(k) for k in range(1, pairs)]

    mine = pl.ds(row * slots, slots)
    loads = [
        pltpu.make_async_copy(up_hbm, up_mat.at[mine], loc_sem.at[2]),
        pltpu.make_async_copy(dn_hbm, dn_mat.at[mine], loc_sem.at[3]),
    ]
    for load in loads:
        load.start()
    home = pl.ds(part * wide, wide)
    for a, (src, dst) in enumerate(((x_hbm, x_all), (y_hbm, y_all))):
        for t in range(chunks):
            for b in range(wide):
                pltpu.make_async_copy(
                    src.at[pl.ds(t * step, step), pl.ds(b * blk, blk)],
                    dst[t].at[part * wide + b], own_sem.at[a, t],
                ).start()
            loads.append(
                pltpu.make_async_copy(dst[t].at[home], dst[t].at[home], own_sem.at[a, t])
            )
    lane = lax.broadcasted_iota(jnp.int32, (8, 128), 1)
    sub = lax.broadcasted_iota(jnp.int32, (8, 128), 0)
    packed = jnp.full((8, 128), -1, jnp.int32)
    for s in range(slots):
        for j, src in enumerate((up_pos, up_pos, dn_pos, dn_pos)):
            packed = jnp.where((sub == s) & (lane == j), src[s, j % 2], packed)
    own_pos[...] = packed
    row_pos[row] = packed

    barrier = pltpu.get_barrier_semaphore()
    for peer in peers:
        pl.semaphore_signal(barrier, inc=1, device_id=peer, device_id_type=MESH)
    pl.semaphore_wait(barrier, len(peers))

    pos_row = []
    for k in range(1, rows):
        copy = remote(own_pos, row_pos.at[row], rp_send.at[k], rp_recv.at[k], row_peer(k))
        copy.start()
        pos_row.append(copy)
    swap = {}
    for t in range(chunks):
        here = pl.ds(t * step, step)
        for a, (src, dst) in enumerate(((x_hbm, x_all), (y_hbm, y_all))):
            for k in range(1, pairs):
                sems = (ex_send.at[a, t, k], ex_recv.at[a, t, k], part_peer(k))
                for b in range(wide):
                    remote(
                        src.at[here, pl.ds(b * blk, blk)],
                        dst[t].at[part * wide + b], *sems,
                    ).start()
                swap[a, t, k] = remote(dst[t].at[home], dst[t].at[home], *sems)
    mats = []
    for a, (src, dst) in enumerate(((up_hbm, up_mat), (dn_hbm, dn_mat))):
        for k in range(1, rows):
            copy = remote(src, dst.at[mine], w_send.at[a, k], w_recv.at[a, k], row_peer(k))
            copy.start()
            mats.append(copy)

    for copy in pos_row:
        copy.wait()
    pos_grp = []
    for k in range(1, rows):
        copy = remote(
            row_pos.at[grp_of(k)], grp_pos.at[group],
            gp_send.at[k], gp_recv.at[k], grp_peer(k),
        )
        copy.start()
        pos_grp.append(copy)
    grp_pos[group] = row_pos[group]
    row_copy = pltpu.make_async_copy(row_pos, row_tab, tab_sem.at[0])
    row_copy.start()
    for copy in pos_grp:
        copy.wait()
    row_copy.wait()
    grp_copy = pltpu.make_async_copy(grp_pos, grp_tab, tab_sem.at[1])
    grp_copy.start()
    grp_copy.wait()
    for load in loads:
        load.wait()

    sel = {}
    for t in range(chunks):
        here = pl.ds(t * step, step)
        for a, (src, out, dst) in enumerate(((x_all, x_out, x_sel), (y_all, y_out, y_sel))):
            for k in range(1, pairs):
                swap[a, t, k].wait_recv()

            def pick(whose, s):
                return src[t][jnp.maximum(grp_tab[whose, s, 3 * a], 0)]

            for k in range(1, rows):
                for s in range(slots):
                    out[k, s, here] = pick(grp_of(k), s)
                copy = remote(
                    out.at[k, :, here], dst.at[pl.ds(group * slots, slots), here],
                    sel_send.at[a, t, k], sel_recv.at[a, t, k], grp_peer(k),
                )
                copy.start()
                sel[a, t, k] = copy
            for s in range(slots):
                dst[group * slots + s, here] = pick(group, s)

    for copy in mats:
        copy.wait_recv()

    def up_col(i):
        return row_tab[i // slots, i % slots, 1]

    def down_row(i):
        return row_tab[i // slots, i % slots, 2]

    back = {}
    for t in range(chunks):
        here = pl.ds(t * step, step)
        for a in range(2):
            for k in range(1, rows):
                sel[a, t, k].wait_recv()

        @pl.loop(0, total)
        def _(i):
            block_out[i] = dot(x_sel[i, here], up_mat[i], 1, 0)
            down_part[i] = dot(y_sel[i, here], dn_mat[i], 1, 1)

        @pl.loop(0, total)
        def _(i):
            spot = up_col(i)
            hidden = jnp.zeros((step, blk), jnp.float32)
            grad = jnp.zeros((step, blk), jnp.float32)
            for j in range(total):
                hidden += flag((up_col(j) == spot) & (spot >= 0)) * block_out[j]
                grad += flag((down_row(j) == spot) & (spot >= 0)) * down_part[j]
            _, slope = gelu_parts(hidden)
            dh = (grad * slope).astype(jnp.bfloat16)
            dhid[i, here] = dh
            back_out[i, here] = dot(dh, up_mat[i], 1, 1).astype(jnp.bfloat16)

        for k in range(1, rows):
            copy = remote(
                back_out.at[pl.ds(grp_of(k) * slots, slots), here],
                back_in.at[pl.ds(group * slots, slots), here],
                bk_send.at[t, k], bk_recv.at[t, k], grp_peer(k),
            )
            copy.start()
            back[t, k] = copy
        for s in range(slots):
            back_in[group * slots + s, here] = back_out[group * slots + s, here]

        @pl.loop(0, total)
        def _(i):
            spot = down_row(i)
            hidden = jnp.zeros((step, blk), jnp.float32)
            for j in range(total):
                hidden += flag((up_col(j) == spot) & (spot >= 0)) * block_out[j]
            value, _ = gelu_parts(hidden)
            act[i, here] = value.astype(jnp.bfloat16)

    @pl.loop(0, total)
    def _(i):
        term = dot(act[i], y_sel[i], 0, 0) * flag(down_row(i) >= 0)
        dn_out[i] = term.astype(jnp.bfloat16)
        term = dot(x_sel[i], dhid[i], 0, 0) * flag(up_col(i) >= 0)
        up_out[i] = term.astype(jnp.bfloat16)

    grads = []
    for a, (src, dst) in enumerate(((up_out, up_in), (dn_out, dn_in))):
        for k in range(1, rows):
            copy = remote(
                src.at[pl.ds(lax.rem(row + k, rows) * slots, slots)], dst.at[k],
                gr_send.at[a, k], gr_recv.at[a, k], row_peer(k),
            )
            copy.start()
            grads.append(copy)

    def gather_block(spot, here):
        summed = jnp.zeros((step, blk), jnp.float32)
        for j in range(total):
            keep = flag(grp_tab[j // slots, j % slots, 0] == spot)
            summed += keep * back_in[j, here].astype(jnp.float32)
        return summed

    fold = {}
    for t in range(chunks):
        here = pl.ds(t * step, step)
        for k in range(1, rows):
            back[t, k].wait_recv()
        for k in range(1, pairs):

            @pl.loop(0, wide)
            def _(b):
                lanes = pl.ds(pl.multiple_of(b * blk, blk), blk)
                value = gather_block(part_of(k) * wide + b, here)
                fold_out[k, here, lanes] = value.astype(jnp.bfloat16)

            copy = remote(
                fold_out.at[k, here], fold_in.at[k, here],
                fx_send.at[t, k], fx_recv.at[t, k], part_peer(k),
            )
            copy.start()
            fold[t, k] = copy

    for copy in grads:
        copy.wait_recv()
    for src, got, dst in ((up_out, up_in, ugrad_ref), (dn_out, dn_in, dgrad_ref)):
        for s in range(slots):
            summed = src[row * slots + s].astype(jnp.float32)
            for k in range(1, rows):
                summed += got[k, s].astype(jnp.float32)
            dst[s] = summed.astype(jnp.bfloat16)

    for t in range(chunks):
        here = pl.ds(t * step, step)
        for k in range(1, pairs):
            fold[t, k].wait_recv()

        @pl.loop(0, wide)
        def _(b):
            lanes = pl.ds(pl.multiple_of(b * blk, blk), blk)
            value = gather_block(part * wide + b, here)
            for k in range(1, pairs):
                value += fold_in[k, here, lanes].astype(jnp.float32)
            gin_ref[here, lanes] = value.astype(jnp.bfloat16)

    for group_of in (swap, sel, back, fold):
        for copy in group_of.values():
            copy.wait_send()
    for copy in mats + grads:
        copy.wait_send()


def body(rows, cols, inputs, grad_out, up_blocks, up_where, down_blocks, down_where):
    pairs = cols // rows
    slots, blk = up_blocks.shape[:2]
    tok, width = inputs.shape
    total = rows * slots
    chunks = CHUNKS
    bf, f32 = jnp.bfloat16, jnp.float32
    dma = pltpu.SemaphoreType.DMA
    vmem, smem = pltpu.VMEM, pltpu.SMEM
    step = tok // chunks
    scratch = [
        vmem((8, 128), jnp.int32),
        vmem((rows, 8, 128), jnp.int32),
        vmem((rows, 8, 128), jnp.int32),
        smem((rows, 8, 128), jnp.int32),
        smem((rows, 8, 128), jnp.int32),
        [vmem((pairs * width // blk, step, blk), bf) for _ in range(chunks)],
        [vmem((pairs * width // blk, step, blk), bf) for _ in range(chunks)],
        vmem((rows, slots, tok, blk), bf),
        vmem((rows, slots, tok, blk), bf),
        vmem((total, tok, blk), bf),
        vmem((total, tok, blk), bf),
        vmem((total, blk, blk), bf),
        vmem((total, blk, blk), bf),
        vmem((total, step, blk), f32),
        vmem((total, step, blk), f32),
        vmem((total, tok, blk), bf),
        vmem((total, tok, blk), bf),
        vmem((total, tok, blk), bf),
        vmem((total, tok, blk), bf),
        vmem((pairs, tok, width), bf),
        vmem((pairs, tok, width), bf),
        vmem((total, blk, blk), bf),
        vmem((rows, slots, blk, blk), bf),
        vmem((total, blk, blk), bf),
        vmem((rows, slots, blk, blk), bf),
        dma((4,)),
        dma((2, chunks)),
        dma((2,)),
    ]
    for shape in (
        (rows,), (rows,), (2, chunks, pairs), (2, rows),
        (2, chunks, rows), (chunks, rows), (chunks, pairs), (2, rows),
    ):
        scratch += [dma(shape), dma(shape)]
    hbm = pl.BlockSpec(memory_space=pl.ANY)
    small = pl.BlockSpec(memory_space=pltpu.SMEM)
    full = pl.BlockSpec(memory_space=pltpu.VMEM)
    return pl.pallas_call(
        functools.partial(kernel, rows, pairs, slots, chunks),
        out_shape=(
            jax.ShapeDtypeStruct(inputs.shape, bf),
            jax.ShapeDtypeStruct(up_blocks.shape, bf),
            jax.ShapeDtypeStruct(down_blocks.shape, bf),
        ),
        in_specs=[hbm, hbm, hbm, hbm, small, small],
        out_specs=(full, full, full),
        scratch_shapes=scratch,
        compiler_params=pltpu.CompilerParams(collective_id=0, has_side_effects=True),
    )(inputs, grad_out, up_blocks, down_blocks, up_where, down_where)


def solution(mesh):
    rows, cols = mesh.shape["row"], mesh.shape["col"]
    placed = (
        P("row", "col"),
        P("row", "col"),
        P("row", "col", None),
        P("row", "col"),
        P("row", "col", None),
        P("row", "col"),
    )
    return jax.shard_map(
        functools.partial(body, rows, cols),
        mesh=mesh,
        in_specs=placed,
        out_specs=(P("row", "col"), P("row", "col", None), P("row", "col", None)),
        check_vma=False,
    )
```

time: 268 us -> 44.5 us (0.17)
  waiting for transfers between devices: 178 us -> 0 us
  Pallas kernels: 0 us -> 40.5 us
  blocking collectives: 25.8 us -> 0 us
  local copies, waits for them, and re-layouts: 28.5 us -> 3.2 us
  other arithmetic: 15.1 us -> 0 us
  between operations: 13.9 us -> 0.65 us
  matrix products: 5.79 us -> 0 us
    reduce_scatter x3 -> x0, waiting for transfers between devices: 106 us -> none  [the longest x1 62.6 us: body(): lax.psum_scatter(partial_value.astype(jnp.bfloat16), 'col', scatter_dimen...]
    all_gather x2 -> x0, waiting for transfers between devices: 71.8 us -> none  [the longest x1 46.6 us: body(): lax.all_gather(grad_out, 'col', axis=1, tiled=True)]
    pallas_call x0 -> x1, Pallas kernels: none -> 40.5 us  [body(): pl.pallas_call(functools.partial(kernel, rows, pairs, slots, chunks), out...]
    all_gather x4 -> x0, blocking collectives: 25.8 us -> none  [the longest x1 7.8 us: body(): lax.all_gather(down_blocks, 'row', axis=0, tiled=True)]
    scatter-add x3 -> x0, other arithmetic: 7.64 us -> none  [the longest x1 2.91 us: body(): jnp.zeros((tok_rows, col_blocks, block_side), jnp.float32).at[:, down_frow]]
    gather x4 -> x0, local copies, waits for them, and re-layouts: 7.57 us -> none  [the longest x1 2.97 us: body(): jnp.take(whole_grad.reshape(tok_rows, d_count, block_side), down_dcol, ax...]
    convert_element_type x2 -> x0, other arithmetic: 7.37 us -> none  [the longest x1 4.82 us: body(): act = value.astype(jnp.bfloat16)]
    reshape x2 -> x0, local copies, waits for them, and re-layouts: 7.29 us -> none  [the longest x1 4.07 us: body(): whole_grad.reshape(tok_rows, d_count, block_side)]
  transfers between devices with their start and end apart: 5 -> 0, of which waited for: 5 -> 0; matrix products, arithmetic and copies ran while one was open for 4% -> 0% of each run, Pallas kernels for 0% -> 0%
where the time goes in v1:
time: 44.5 us; the launch traced here: 44.3 us
  Pallas kernels  40.5 us (91%)
  local copies, waits for them, and re-layouts  3.2 us (7%)
  between operations  0.65 us (1%)
    pallas_call x1, Pallas kernels, body(): pl.pallas_call(functools.partial(kernel, rows, pairs, slots, chunks), out...  40.5 us
    unnamed x7, local copies, waits for them, and re-layouts  3.2 us

profile of v1, /device:TPU:0, one launch (start us, length us, event | category | flops | bytes accessed | tf_op | source)
XLA Modules:
  0.0 44.3 jit_solution(13375930365028471479)
XLA Ops:
  0.6 40.5 %shard_map.85 = (bf16[128,1024]{1,0:T(8,128)(2,1)}, bf16[2,128,128]{2,1,0:T(8,128)(2,1)}, bf16[2,128,128]{2,1,0:T(8,128)(2,1)}) custom-call(bf16[128,1024]{1,0:T(8,128)(2,1)} %x_hbm.1, bf16[128,1024]{1,0:T(8,128)(2,1)} %y_hbm.1, bf16[2,128,128]{2,1,0:T(8,128)(2,1)} %up_hbm.1, bf16[2,128,128]{2,1,0:T(8,128)(2,1)} %dn_hbm.1, s32[2,2]{1,0:T(2,128)} %up_pos.1, ...), custom_call_target="tpu_custom_call" | custom-call | tf_op jit(solution)/shard_map/pallas_call | solution.py:358
  41.1 0.0 copy-start.1
  41.1 1.7 %copy.12 = bf16[128,1024]{1,0:T(8,128)(2,1)} copy(bf16[128,1024]{1,0:T(8,128)(2,1)} %get-tuple-element.6) | data formatting | bytes 524288
  42.8 0.0 copy-done.1
  42.8 0.0 copy-start
  42.8 0.6 %copy.13 = bf16[2,128,128]{2,1,0:T(8,128)(2,1)} copy(bf16[2,128,128]{2,1,0:T(8,128)(2,1)S(1)} %copy-done.1) | data formatting | bytes 131072
  43.5 0.2 copy-done
  43.7 0.6 %copy.14 = bf16[2,128,128]{2,1,0:T(8,128)(2,1)} copy(bf16[2,128,128]{2,1,0:T(8,128)(2,1)S(1)} %copy-done) | data formatting | bytes 131072
Async XLA Ops:
  41.1 1.7 %copy-start.1 = (bf16[2,128,128]{2,1,0:T(8,128)(2,1)S(1)}, bf16[2,128,128]{2,1,0:T(8,128)(2,1)}, u32[]{:S(2)}) copy-start(bf16[2,128,128]{2,1,0:T(8,128)(2,1)} %get-tuple-element.7) | copy-start | bytes 196612
  42.8 0.9 %copy-start = (bf16[2,128,128]{2,1,0:T(8,128)(2,1)S(1)}, bf16[2,128,128]{2,1,0:T(8,128)(2,1)}, u32[]{:S(2)}) copy-start(bf16[2,128,128]{2,1,0:T(8,128)(2,1)} %get-tuple-element.8) | copy-start | bytes 196612

commit v2 on v1

--- a/solution.py
+++ b/solution.py
@@ -8,7 +8,7 @@
 from jax.sharding import PartitionSpec as P
 
 MESH = pl.DeviceIdType.MESH
-CHUNKS = 2
+CHUNKS = 4
 
 
 def gelu_parts(hidden):
@@ -35,11 +35,11 @@
 
 def kernel(
     rows, pairs, slots, chunks,
-    x_hbm, y_hbm, up_hbm, dn_hbm, up_pos, dn_pos,
+    x_hbm, y_hbm, up_hbm, dn_hbm, up_hpos, dn_hpos,
     gin_ref, ugrad_ref, dgrad_ref,
-    own_pos, row_pos, grp_pos, row_tab, grp_tab,
+    up_pos, dn_pos, own_pos, row_pos, grp_pos, row_tab, grp_tab,
     x_all, y_all, x_out, y_out, x_sel, y_sel,
-    up_mat, dn_mat, block_out, down_part, act, dhid,
+    up_mat, dn_mat, block_out, down_part, home_sum, dhid,
     back_out, back_in, fold_out, fold_in,
     up_out, up_in, dn_out, dn_in,
     loc_sem, own_sem, tab_sem,
@@ -79,6 +79,16 @@
     peers = [row_peer(k) for k in range(1, rows)]
     peers += [grp_peer(k) for k in range(1, rows)]
     peers += [part_peer(k) for k in range(1, pairs)]
+
+    barrier = pltpu.get_barrier_semaphore()
+    for peer in peers:
+        pl.semaphore_signal(barrier, inc=1, device_id=peer, device_id_type=MESH)
+    tables = [
+        pltpu.make_async_copy(up_hpos, up_pos, tab_sem.at[2]),
+        pltpu.make_async_copy(dn_hpos, dn_pos, tab_sem.at[3]),
+    ]
+    for table in tables:
+        table.start()
 
     mine = pl.ds(row * slots, slots)
     loads = [
@@ -98,6 +108,8 @@
             loads.append(
                 pltpu.make_async_copy(dst[t].at[home], dst[t].at[home], own_sem.at[a, t])
             )
+    for table in tables:
+        table.wait()
     lane = lax.broadcasted_iota(jnp.int32, (8, 128), 1)
     sub = lax.broadcasted_iota(jnp.int32, (8, 128), 0)
     packed = jnp.full((8, 128), -1, jnp.int32)
@@ -107,9 +119,6 @@
     own_pos[...] = packed
     row_pos[row] = packed
 
-    barrier = pltpu.get_barrier_semaphore()
-    for peer in peers:
-        pl.semaphore_signal(barrier, inc=1, device_id=peer, device_id_type=MESH)
     pl.semaphore_wait(barrier, len(peers))
 
     pos_row = []
@@ -189,7 +198,41 @@
     def down_row(i):
         return row_tab[i // slots, i % slots, 2]
 
-    back = {}
+    def gather_block(spot, t):
+        here = pl.ds(t * step, step)
+        summed = jnp.zeros((step, blk), jnp.float32)
+        for j in range(total):
+            keep = flag(grp_tab[j // slots, j % slots, 0] == spot)
+            summed += keep * back_in[j, here].astype(jnp.float32)
+        return summed
+
+    back, fold = {}, {}
+
+    def send_fold(t):
+        here = pl.ds(t * step, step)
+        for k in range(1, rows):
+            back[t, k].wait_recv()
+        for k in range(1, pairs):
+
+            @pl.loop(0, wide)
+            def _(b):
+                lanes = pl.ds(pl.multiple_of(b * blk, blk), blk)
+                value = gather_block(part_of(k) * wide + b, t)
+                fold_out[k, here, lanes] = value.astype(jnp.bfloat16)
+
+            copy = remote(
+                fold_out.at[k, here], fold_in.at[k, here],
+                fx_send.at[t, k], fx_recv.at[t, k], part_peer(k),
+            )
+            copy.start()
+            fold[t, k] = copy
+
+    def sum_home(t):
+        @pl.loop(0, wide)
+        def _(b):
+            lanes = pl.ds(pl.multiple_of(b * blk, blk), blk)
+            home_sum[pl.ds(t * step, step), lanes] = gather_block(part * wide + b, t)
+
     for t in range(chunks):
         here = pl.ds(t * step, step)
         for a in range(2):
@@ -198,7 +241,7 @@
 
         @pl.loop(0, total)
         def _(i):
-            block_out[i] = dot(x_sel[i, here], up_mat[i], 1, 0)
+            block_out[i, here] = dot(x_sel[i, here], up_mat[i], 1, 0)
             down_part[i] = dot(y_sel[i, here], dn_mat[i], 1, 1)
 
         @pl.loop(0, total)
@@ -207,7 +250,7 @@
             hidden = jnp.zeros((step, blk), jnp.float32)
             grad = jnp.zeros((step, blk), jnp.float32)
             for j in range(total):
-                hidden += flag((up_col(j) == spot) & (spot >= 0)) * block_out[j]
+                hidden += flag((up_col(j) == spot) & (spot >= 0)) * block_out[j, here]
                 grad += flag((down_row(j) == spot) & (spot >= 0)) * down_part[j]
             _, slope = gelu_parts(hidden)
             dh = (grad * slope).astype(jnp.bfloat16)
@@ -224,19 +267,18 @@
             back[t, k] = copy
         for s in range(slots):
             back_in[group * slots + s, here] = back_out[group * slots + s, here]
-
-        @pl.loop(0, total)
-        def _(i):
-            spot = down_row(i)
-            hidden = jnp.zeros((step, blk), jnp.float32)
-            for j in range(total):
-                hidden += flag((up_col(j) == spot) & (spot >= 0)) * block_out[j]
-            value, _ = gelu_parts(hidden)
-            act[i, here] = value.astype(jnp.bfloat16)
+        if t > 0:
+            send_fold(t - 1)
 
     @pl.loop(0, total)
     def _(i):
-        term = dot(act[i], y_sel[i], 0, 0) * flag(down_row(i) >= 0)
+        spot = down_row(i)
+        hidden = jnp.zeros((tok, blk), jnp.float32)
+        for j in range(total):
+            hidden += flag((up_col(j) == spot) & (spot >= 0)) * block_out[j]
+        value, _ = gelu_parts(hidden)
+        act = value.astype(jnp.bfloat16)
+        term = dot(act, y_sel[i], 0, 0) * flag(spot >= 0)
         dn_out[i] = term.astype(jnp.bfloat16)
         term = dot(x_sel[i], dhid[i], 0, 0) * flag(up_col(i) >= 0)
         up_out[i] = term.astype(jnp.bfloat16)
@@ -251,32 +293,17 @@
             copy.start()
             grads.append(copy)
 
-    def gather_block(spot, here):
-        summed = jnp.zeros((step, blk), jnp.float32)
-        for j in range(total):
-            keep = flag(grp_tab[j // slots, j % slots, 0] == spot)
-            summed += keep * back_in[j, here].astype(jnp.float32)
-        return summed
-
-    fold = {}
+    send_fold(chunks - 1)
     for t in range(chunks):
-        here = pl.ds(t * step, step)
-        for k in range(1, rows):
-            back[t, k].wait_recv()
+        sum_home(t)
+
+    for t in range(chunks):
+        here = pl.ds(t * step, step)
+        value = home_sum[here]
         for k in range(1, pairs):
-
-            @pl.loop(0, wide)
-            def _(b):
-                lanes = pl.ds(pl.multiple_of(b * blk, blk), blk)
-                value = gather_block(part_of(k) * wide + b, here)
-                fold_out[k, here, lanes] = value.astype(jnp.bfloat16)
-
-            copy = remote(
-                fold_out.at[k, here], fold_in.at[k, here],
-                fx_send.at[t, k], fx_recv.at[t, k], part_peer(k),
-            )
-            copy.start()
-            fold[t, k] = copy
+            fold[t, k].wait_recv()
+            value += fold_in[k, here].astype(jnp.float32)
+        gin_ref[here] = value.astype(jnp.bfloat16)
 
     for copy in grads:
         copy.wait_recv()
@@ -286,19 +313,6 @@
             for k in range(1, rows):
                 summed += got[k, s].astype(jnp.float32)
             dst[s] = summed.astype(jnp.bfloat16)
-
-    for t in range(chunks):
-        here = pl.ds(t * step, step)
-        for k in range(1, pairs):
-            fold[t, k].wait_recv()
-
-        @pl.loop(0, wide)
-        def _(b):
-            lanes = pl.ds(pl.multiple_of(b * blk, blk), blk)
-            value = gather_block(part * wide + b, here)
-            for k in range(1, pairs):
-                value += fold_in[k, here, lanes].astype(jnp.float32)
-            gin_ref[here, lanes] = value.astype(jnp.bfloat16)
 
     for group_of in (swap, sel, back, fold):
         for copy in group_of.values():
@@ -318,6 +332,8 @@
     vmem, smem = pltpu.VMEM, pltpu.SMEM
     step = tok // chunks
     scratch = [
+        smem((slots, 2), jnp.int32),
+        smem((slots, 2), jnp.int32),
         vmem((8, 128), jnp.int32),
         vmem((rows, 8, 128), jnp.int32),
         vmem((rows, 8, 128), jnp.int32),
@@ -331,9 +347,9 @@
         vmem((total, tok, blk), bf),
         vmem((total, blk, blk), bf),
         vmem((total, blk, blk), bf),
+        vmem((total, tok, blk), f32),
         vmem((total, step, blk), f32),
-        vmem((total, step, blk), f32),
-        vmem((total, tok, blk), bf),
+        vmem((tok, width), f32),
         vmem((total, tok, blk), bf),
         vmem((total, tok, blk), bf),
         vmem((total, tok, blk), bf),
@@ -345,7 +361,7 @@
         vmem((rows, slots, blk, blk), bf),
         dma((4,)),
         dma((2, chunks)),
-        dma((2,)),
+        dma((4,)),
     ]
     for shape in (
         (rows,), (rows,), (2, chunks, pairs), (2, rows),
@@ -353,7 +369,6 @@
     ):
         scratch += [dma(shape), dma(shape)]
     hbm = pl.BlockSpec(memory_space=pl.ANY)
-    small = pl.BlockSpec(memory_space=pltpu.SMEM)
     full = pl.BlockSpec(memory_space=pltpu.VMEM)
     return pl.pallas_call(
         functools.partial(kernel, rows, pairs, slots, chunks),
@@ -362,7 +377,7 @@
             jax.ShapeDtypeStruct(up_blocks.shape, bf),
             jax.ShapeDtypeStruct(down_blocks.shape, bf),
         ),
-        in_specs=[hbm, hbm, hbm, hbm, small, small],
+        in_specs=[hbm] * 6,
         out_specs=(full, full, full),
         scratch_shapes=scratch,
         compiler_params=pltpu.CompilerParams(collective_id=0, has_side_effects=True),

time: 44.5 us -> 46.9 us (1.054)
  Pallas kernels: 40.5 us -> 42.8 us
    pallas_call x1, Pallas kernels: 40.5 us -> 42.8 us  [body(): pl.pallas_call(functools.partial(kernel, rows, pairs, slots, chunks), out...]
where the time goes in v2:
time: 46.9 us; the launch traced here: 46.7 us
  Pallas kernels  42.8 us (91%)
  local copies, waits for them, and re-layouts  3.2 us (7%)
  between operations  0.65 us (1%)
    pallas_call x1, Pallas kernels, body(): pl.pallas_call(functools.partial(kernel, rows, pairs, slots, chunks), out...  42.8 us
    unnamed x7, local copies, waits for them, and re-layouts  3.2 us

profile of v2, /device:TPU:0, one launch (start us, length us, event | category | flops | bytes accessed | tf_op | source)
XLA Modules:
  0.0 46.7 jit_solution(8012260635057510026)
XLA Ops:
  0.6 42.8 %shard_map.85 = (bf16[128,1024]{1,0:T(8,128)(2,1)}, bf16[2,128,128]{2,1,0:T(8,128)(2,1)}, bf16[2,128,128]{2,1,0:T(8,128)(2,1)}) custom-call(bf16[128,1024]{1,0:T(8,128)(2,1)} %x_hbm.1, bf16[128,1024]{1,0:T(8,128)(2,1)} %y_hbm.1, bf16[2,128,128]{2,1,0:T(8,128)(2,1)} %up_hbm.1, bf16[2,128,128]{2,1,0:T(8,128)(2,1)} %dn_hbm.1, s32[2,2]{1,0:T(2,128)} %up_hpos.1, ...), custom_call_target="tpu_custom_call" | custom-call | tf_op jit(solution)/shard_map/pallas_call | solution.py:373
  43.5 0.0 copy-start.1
  43.5 1.7 %copy.12 = bf16[128,1024]{1,0:T(8,128)(2,1)} copy(bf16[128,1024]{1,0:T(8,128)(2,1)} %get-tuple-element.6) | data formatting | bytes 524288
  45.2 0.0 copy-done.1
  45.2 0.0 copy-start
  45.2 0.6 %copy.13 = bf16[2,128,128]{2,1,0:T(8,128)(2,1)} copy(bf16[2,128,128]{2,1,0:T(8,128)(2,1)S(1)} %copy-done.1) | data formatting | bytes 131072
  45.8 0.2 copy-done
  46.1 0.6 %copy.14 = bf16[2,128,128]{2,1,0:T(8,128)(2,1)} copy(bf16[2,128,128]{2,1,0:T(8,128)(2,1)S(1)} %copy-done) | data formatting | bytes 131072
Async XLA Ops:
  43.5 1.7 %copy-start.1 = (bf16[2,128,128]{2,1,0:T(8,128)(2,1)S(1)}, bf16[2,128,128]{2,1,0:T(8,128)(2,1)}, u32[]{:S(2)}) copy-start(bf16[2,128,128]{2,1,0:T(8,128)(2,1)} %get-tuple-element.7) | copy-start | bytes 196612
  45.2 0.9 %copy-start = (bf16[2,128,128]{2,1,0:T(8,128)(2,1)S(1)}, bf16[2,128,128]{2,1,0:T(8,128)(2,1)}, u32[]{:S(2)}) copy-start(bf16[2,128,128]{2,1,0:T(8,128)(2,1)} %get-tuple-element.8) | copy-start | bytes 196612

commit v3 on v2

--- a/solution.py
+++ b/solution.py
@@ -8,7 +8,7 @@
 from jax.sharding import PartitionSpec as P
 
 MESH = pl.DeviceIdType.MESH
-CHUNKS = 4
+CHUNKS = 2
 
 
 def gelu_parts(hidden):

time: 46.9 us -> 43.6 us (0.930)
  Pallas kernels: 42.8 us -> 39.5 us
    pallas_call x1, Pallas kernels: 42.8 us -> 39.5 us  [body(): pl.pallas_call(functools.partial(kernel, rows, pairs, slots, chunks), out...]
where the time goes in v3:
time: 43.6 us; the launch traced here: 43.4 us
  Pallas kernels  39.5 us (91%)
  local copies, waits for them, and re-layouts  3.2 us (7%)
  between operations  0.65 us (1%)
    pallas_call x1, Pallas kernels, body(): pl.pallas_call(functools.partial(kernel, rows, pairs, slots, chunks), out...  39.5 us
    unnamed x7, local copies, waits for them, and re-layouts  3.2 us

profile of v3, /device:TPU:0, one launch (start us, length us, event | category | flops | bytes accessed | tf_op | source)
XLA Modules:
  0.0 43.4 jit_solution(15843974044289767134)
XLA Ops:
  0.6 39.5 %shard_map.85 = (bf16[128,1024]{1,0:T(8,128)(2,1)}, bf16[2,128,128]{2,1,0:T(8,128)(2,1)}, bf16[2,128,128]{2,1,0:T(8,128)(2,1)}) custom-call(bf16[128,1024]{1,0:T(8,128)(2,1)} %x_hbm.1, bf16[128,1024]{1,0:T(8,128)(2,1)} %y_hbm.1, bf16[2,128,128]{2,1,0:T(8,128)(2,1)} %up_hbm.1, bf16[2,128,128]{2,1,0:T(8,128)(2,1)} %dn_hbm.1, s32[2,2]{1,0:T(2,128)} %up_hpos.1, ...), custom_call_target="tpu_custom_call" | custom-call | tf_op jit(solution)/shard_map/pallas_call | solution.py:373
  40.2 0.0 copy-start.1
  40.2 1.7 %copy.12 = bf16[128,1024]{1,0:T(8,128)(2,1)} copy(bf16[128,1024]{1,0:T(8,128)(2,1)} %get-tuple-element.6) | data formatting | bytes 524288
  41.9 0.0 copy-done.1
  41.9 0.0 copy-start
  41.9 0.6 %copy.13 = bf16[2,128,128]{2,1,0:T(8,128)(2,1)} copy(bf16[2,128,128]{2,1,0:T(8,128)(2,1)S(1)} %copy-done.1) | data formatting | bytes 131072
  42.5 0.2 copy-done
  42.8 0.6 %copy.14 = bf16[2,128,128]{2,1,0:T(8,128)(2,1)} copy(bf16[2,128,128]{2,1,0:T(8,128)(2,1)S(1)} %copy-done) | data formatting | bytes 131072
Async XLA Ops:
  40.2 1.7 %copy-start.1 = (bf16[2,128,128]{2,1,0:T(8,128)(2,1)S(1)}, bf16[2,128,128]{2,1,0:T(8,128)(2,1)}, u32[]{:S(2)}) copy-start(bf16[2,128,128]{2,1,0:T(8,128)(2,1)} %get-tuple-element.7) | copy-start | bytes 196612
  41.9 0.9 %copy-start = (bf16[2,128,128]{2,1,0:T(8,128)(2,1)S(1)}, bf16[2,128,128]{2,1,0:T(8,128)(2,1)}, u32[]{:S(2)}) copy-start(bf16[2,128,128]{2,1,0:T(8,128)(2,1)} %get-tuple-element.8) | copy-start | bytes 196612

commit v4 on v3

--- a/solution.py
+++ b/solution.py
@@ -27,6 +27,23 @@
         left, right, (((left_dim,), (right_dim,)), ((), ())),
         preferred_element_type=jnp.float32,
     )
+
+
+def each(count, unroll=8):
+    size = max(n for n in range(1, unroll + 1) if count % n == 0)
+
+    def run(body):
+        if size == count:
+            for i in range(count):
+                body(i)
+            return
+
+        @pl.loop(0, count // size)
+        def _(outer):
+            for i in range(size):
+                body(outer * size + i)
+
+    return run
 
 
 def flag(pred):
@@ -239,12 +256,12 @@
             for k in range(1, rows):
                 sel[a, t, k].wait_recv()
 
-        @pl.loop(0, total)
+        @each(total)
         def _(i):
             block_out[i, here] = dot(x_sel[i, here], up_mat[i], 1, 0)
             down_part[i] = dot(y_sel[i, here], dn_mat[i], 1, 1)
 
-        @pl.loop(0, total)
+        @each(total)
         def _(i):
             spot = up_col(i)
             hidden = jnp.zeros((step, blk), jnp.float32)
@@ -270,7 +287,7 @@
         if t > 0:
             send_fold(t - 1)
 
-    @pl.loop(0, total)
+    @each(total)
     def _(i):
         spot = down_row(i)
         hidden = jnp.zeros((tok, blk), jnp.float32)

time: 43.6 us -> 42 us (0.963)
  Pallas kernels: 39.5 us -> 37.9 us
    pallas_call x1, Pallas kernels: 39.5 us -> 37.9 us  [body(): pl.pallas_call(functools.partial(kernel, rows, pairs, slots, chunks), out...]
where the time goes in v4:
time: 42 us; the launch traced here: 41.7 us
  Pallas kernels  37.9 us (90%)
  local copies, waits for them, and re-layouts  3.2 us (8%)
  between operations  0.65 us (2%)
    pallas_call x1, Pallas kernels, body(): pl.pallas_call(functools.partial(kernel, rows, pairs, slots, chunks), out...  37.9 us
    unnamed x7, local copies, waits for them, and re-layouts  3.2 us

profile of v4, /device:TPU:0, one launch (start us, length us, event | category | flops | bytes accessed | tf_op | source)
XLA Modules:
  0.0 41.7 jit_solution(7075077847797215153)
XLA Ops:
  0.6 37.9 %shard_map.85 = (bf16[128,1024]{1,0:T(8,128)(2,1)}, bf16[2,128,128]{2,1,0:T(8,128)(2,1)}, bf16[2,128,128]{2,1,0:T(8,128)(2,1)}) custom-call(bf16[128,1024]{1,0:T(8,128)(2,1)} %x_hbm.1, bf16[128,1024]{1,0:T(8,128)(2,1)} %y_hbm.1, bf16[2,128,128]{2,1,0:T(8,128)(2,1)} %up_hbm.1, bf16[2,128,128]{2,1,0:T(8,128)(2,1)} %dn_hbm.1, s32[2,2]{1,0:T(2,128)} %up_hpos.1, ...), custom_call_target="tpu_custom_call" | custom-call | tf_op jit(solution)/shard_map/pallas_call | solution.py:390
  38.5 0.0 copy-start.1
  38.5 1.7 %copy.12 = bf16[128,1024]{1,0:T(8,128)(2,1)} copy(bf16[128,1024]{1,0:T(8,128)(2,1)} %get-tuple-element.6) | data formatting | bytes 524288
  40.2 0.0 copy-done.1
  40.2 0.0 copy-start
  40.2 0.6 %copy.13 = bf16[2,128,128]{2,1,0:T(8,128)(2,1)} copy(bf16[2,128,128]{2,1,0:T(8,128)(2,1)S(1)} %copy-done.1) | data formatting | bytes 131072
  40.9 0.2 copy-done
  41.1 0.6 %copy.14 = bf16[2,128,128]{2,1,0:T(8,128)(2,1)} copy(bf16[2,128,128]{2,1,0:T(8,128)(2,1)S(1)} %copy-done) | data formatting | bytes 131072
Async XLA Ops:
  38.5 1.7 %copy-start.1 = (bf16[2,128,128]{2,1,0:T(8,128)(2,1)S(1)}, bf16[2,128,128]{2,1,0:T(8,128)(2,1)}, u32[]{:S(2)}) copy-start(bf16[2,128,128]{2,1,0:T(8,128)(2,1)} %get-tuple-element.7) | copy-start | bytes 196612
  40.2 0.9 %copy-start = (bf16[2,128,128]{2,1,0:T(8,128)(2,1)S(1)}, bf16[2,128,128]{2,1,0:T(8,128)(2,1)}, u32[]{:S(2)}) copy-start(bf16[2,128,128]{2,1,0:T(8,128)(2,1)} %get-tuple-element.8) | copy-start | bytes 196612

commit v5 on v4

--- a/solution.py
+++ b/solution.py
@@ -93,13 +93,31 @@
             device_id=peer, device_id_type=MESH,
         )
 
+    def pick_peer(k):
+        return (lax.rem(row + k, rows), row * pairs + part)
+
+    def pick_source(k):
+        return (group, grp_of(k) * pairs + part)
+
     peers = [row_peer(k) for k in range(1, rows)]
     peers += [grp_peer(k) for k in range(1, rows)]
     peers += [part_peer(k) for k in range(1, pairs)]
 
     barrier = pltpu.get_barrier_semaphore()
+
+    def greet(peer):
+        pl.semaphore_signal(barrier, inc=1, device_id=peer, device_id_type=MESH)
+
+    for k in range(1, rows):
+        greet(pick_source(k))
+
+    @pl.when(row != group)
+    def _():
+        greet(pick_source(0))
+
     for peer in peers:
-        pl.semaphore_signal(barrier, inc=1, device_id=peer, device_id_type=MESH)
+        greet(peer)
+    others = jnp.where(row != group, rows, rows - 1)
     tables = [
         pltpu.make_async_copy(up_hpos, up_pos, tab_sem.at[2]),
         pltpu.make_async_copy(dn_hpos, dn_pos, tab_sem.at[3]),
@@ -136,7 +154,29 @@
     own_pos[...] = packed
     row_pos[row] = packed
 
-    pl.semaphore_wait(barrier, len(peers))
+    pl.semaphore_wait(barrier, len(peers) + others)
+
+    def pos_grp(k):
+        return remote(
+            own_pos, grp_pos.at[group], gp_send.at[k], gp_recv.at[group], pick_peer(k)
+        )
+
+    def pos_grp_in(k):
+        whose = grp_of(k)
+        return remote(
+            own_pos, grp_pos.at[whose], gp_send.at[k], gp_recv.at[whose], pick_peer(k)
+        )
+
+    for k in range(1, rows):
+        pos_grp(k).start()
+
+    @pl.when(row != group)
+    def _():
+        pos_grp(0).start()
+
+    @pl.when(row == group)
+    def _():
+        grp_pos[group] = packed
 
     pos_row = []
     for k in range(1, rows):
@@ -162,22 +202,13 @@
             copy.start()
             mats.append(copy)
 
-    for copy in pos_row:
-        copy.wait()
-    pos_grp = []
     for k in range(1, rows):
-        copy = remote(
-            row_pos.at[grp_of(k)], grp_pos.at[group],
-            gp_send.at[k], gp_recv.at[k], grp_peer(k),
-        )
-        copy.start()
-        pos_grp.append(copy)
-    grp_pos[group] = row_pos[group]
-    row_copy = pltpu.make_async_copy(row_pos, row_tab, tab_sem.at[0])
-    row_copy.start()
-    for copy in pos_grp:
-        copy.wait()
-    row_copy.wait()
+        pos_grp_in(k).wait_recv()
+
+    @pl.when(row != group)
+    def _():
+        pos_grp_in(0).wait_recv()
+
     grp_copy = pltpu.make_async_copy(grp_pos, grp_tab, tab_sem.at[1])
     grp_copy.start()
     grp_copy.wait()
@@ -206,8 +237,13 @@
             for s in range(slots):
                 dst[group * slots + s, here] = pick(group, s)
 
+    for copy in pos_row:
+        copy.wait()
+    row_copy = pltpu.make_async_copy(row_pos, row_tab, tab_sem.at[0])
+    row_copy.start()
     for copy in mats:
         copy.wait_recv()
+    row_copy.wait()
 
     def up_col(i):
         return row_tab[i // slots, i % slots, 1]
@@ -330,6 +366,13 @@
             for k in range(1, rows):
                 summed += got[k, s].astype(jnp.float32)
             dst[s] = summed.astype(jnp.bfloat16)
+
+    for k in range(1, rows):
+        pos_grp(k).wait_send()
+
+    @pl.when(row != group)
+    def _():
+        pos_grp(0).wait_send()
 
     for group_of in (swap, sel, back, fold):
         for copy in group_of.values():
@@ -390,9 +433,9 @@
     return pl.pallas_call(
         functools.partial(kernel, rows, pairs, slots, chunks),
         out_shape=(
-            jax.ShapeDtypeStruct(inputs.shape, bf),
-            jax.ShapeDtypeStruct(up_blocks.shape, bf),
-            jax.ShapeDtypeStruct(down_blocks.shape, bf),
+            vmem(inputs.shape, bf),
+            vmem(up_blocks.shape, bf),
+            vmem(down_blocks.shape, bf),
         ),
         in_specs=[hbm] * 6,
         out_specs=(full, full, full),

time: 42 us -> 38.7 us (0.921)
  Pallas kernels: 37.9 us -> 35.9 us
  local copies, waits for them, and re-layouts: 3.2 us -> 1.96 us
    pallas_call x1, Pallas kernels: 37.9 us -> 35.9 us  [body(): pl.pallas_call(functools.partial(kernel, rows, pairs, slots, chunks), out...]
    unnamed x7 -> x3, local copies, waits for them, and re-layouts: 3.2 us -> 1.96 us
where the time goes in v5:
time: 38.7 us; the launch traced here: 38.5 us
  Pallas kernels  35.9 us (93%)
  local copies, waits for them, and re-layouts  1.96 us (5%)
  between operations  0.64 us (2%)
    pallas_call x1, Pallas kernels, body(): pl.pallas_call(functools.partial(kernel, rows, pairs, slots, chunks), out...  35.9 us
    unnamed x3, local copies, waits for them, and re-layouts  1.96 us

profile of v5, /device:TPU:0, one launch (start us, length us, event | category | flops | bytes accessed | tf_op | source)
XLA Modules:
  0.0 38.5 jit_solution(8854467817748955177)
XLA Ops:
  0.6 35.9 %shard_map.85 = (bf16[128,1024]{1,0:T(8,128)(2,1)S(1)}, bf16[2,128,128]{2,1,0:T(8,128)(2,1)S(1)}, bf16[2,128,128]{2,1,0:T(8,128)(2,1)S(1)}) custom-call(bf16[128,1024]{1,0:T(8,128)(2,1)} %x_hbm.1, bf16[128,1024]{1,0:T(8,128)(2,1)} %y_hbm.1, bf16[2,128,128]{2,1,0:T(8,128)(2,1)} %up_hbm.1, bf16[2,128,128]{2,1,0:T(8,128)(2,1)} %dn_hbm.1, s32[2,2]{1,0:T(2,128)} %up_hpos.1, ...), custom_call_target="tpu_custom_call" | custom-call | tf_op jit(solution)/shard_map/pallas_call | solution.py:433
  36.6 0.7 %copy.12 = bf16[128,1024]{1,0:T(8,128)(2,1)} copy(bf16[128,1024]{1,0:T(8,128)(2,1)S(1)} %get-tuple-element.3) | data formatting | bytes 524288
  37.3 0.6 %copy.13 = bf16[2,128,128]{2,1,0:T(8,128)(2,1)} copy(bf16[2,128,128]{2,1,0:T(8,128)(2,1)S(1)} %get-tuple-element.4) | data formatting | bytes 131072
  37.9 0.6 %copy.14 = bf16[2,128,128]{2,1,0:T(8,128)(2,1)} copy(bf16[2,128,128]{2,1,0:T(8,128)(2,1)S(1)} %get-tuple-element.5) | data formatting | bytes 131072

commit v6 on v5

--- a/solution.py
+++ b/solution.py
@@ -9,6 +9,7 @@
 
 MESH = pl.DeviceIdType.MESH
 CHUNKS = 2
+PIECES = 2
 
 
 def gelu_parts(hidden):
@@ -51,12 +52,12 @@
 
 
 def kernel(
-    rows, pairs, slots, chunks,
+    rows, pairs, slots, chunks, pieces,
     x_hbm, y_hbm, up_hbm, dn_hbm, up_hpos, dn_hpos,
     gin_ref, ugrad_ref, dgrad_ref,
     up_pos, dn_pos, own_pos, row_pos, grp_pos, row_tab, grp_tab,
     x_all, y_all, x_out, y_out, x_sel, y_sel,
-    up_mat, dn_mat, block_out, down_part, home_sum, dhid,
+    up_mat, dn_mat, block_out, down_part, slope_at, home_sum, act, dhid,
     back_out, back_in, fold_out, fold_in,
     up_out, up_in, dn_out, dn_in,
     loc_sem, own_sem, tab_sem,
@@ -70,6 +71,7 @@
     blk = up_hbm.shape[1]
     wide = x_hbm.shape[1] // blk
     step = tok // chunks
+    part_step = step // pieces
     total = rows * slots
 
     def row_peer(k):
@@ -216,34 +218,36 @@
         load.wait()
 
     sel = {}
-    for t in range(chunks):
+
+    def pick_send(t, a):
         here = pl.ds(t * step, step)
-        for a, (src, out, dst) in enumerate(((x_all, x_out, x_sel), (y_all, y_out, y_sel))):
-            for k in range(1, pairs):
-                swap[a, t, k].wait_recv()
-
-            def pick(whose, s):
-                return src[t][jnp.maximum(grp_tab[whose, s, 3 * a], 0)]
-
-            for k in range(1, rows):
-                for s in range(slots):
-                    out[k, s, here] = pick(grp_of(k), s)
-                copy = remote(
-                    out.at[k, :, here], dst.at[pl.ds(group * slots, slots), here],
-                    sel_send.at[a, t, k], sel_recv.at[a, t, k], grp_peer(k),
-                )
-                copy.start()
-                sel[a, t, k] = copy
+        src, out, dst = ((x_all, x_out, x_sel), (y_all, y_out, y_sel))[a]
+        for k in range(1, pairs):
+            swap[a, t, k].wait_recv()
+
+        def pick(whose, s):
+            return src[t][jnp.maximum(grp_tab[whose, s, 3 * a], 0)]
+
+        for k in range(1, rows):
             for s in range(slots):
-                dst[group * slots + s, here] = pick(group, s)
-
-    for copy in pos_row:
-        copy.wait()
-    row_copy = pltpu.make_async_copy(row_pos, row_tab, tab_sem.at[0])
-    row_copy.start()
-    for copy in mats:
-        copy.wait_recv()
-    row_copy.wait()
+                out[k, s, here] = pick(grp_of(k), s)
+            copy = remote(
+                out.at[k, :, here], dst.at[pl.ds(group * slots, slots), here],
+                sel_send.at[a, t, k], sel_recv.at[a, t, k], grp_peer(k),
+            )
+            copy.start()
+            sel[a, t, k] = copy
+        for s in range(slots):
+            dst[group * slots + s, here] = pick(group, s)
+
+    def wait_mats():
+        for copy in pos_row:
+            copy.wait()
+        row_copy = pltpu.make_async_copy(row_pos, row_tab, tab_sem.at[0])
+        row_copy.start()
+        for copy in mats:
+            copy.wait_recv()
+        row_copy.wait()
 
     def up_col(i):
         return row_tab[i // slots, i % slots, 1]
@@ -251,93 +255,90 @@
     def down_row(i):
         return row_tab[i // slots, i % slots, 2]
 
-    def gather_block(spot, t):
-        here = pl.ds(t * step, step)
-        summed = jnp.zeros((step, blk), jnp.float32)
+    def rows_of(piece):
+        return pl.ds(piece * part_step, part_step)
+
+    def gather_block(spot, piece):
+        summed = jnp.zeros((part_step, blk), jnp.float32)
         for j in range(total):
             keep = flag(grp_tab[j // slots, j % slots, 0] == spot)
-            summed += keep * back_in[j, here].astype(jnp.float32)
+            summed += keep * back_in[j, rows_of(piece)].astype(jnp.float32)
         return summed
 
-    back, fold = {}, {}
-
-    def send_fold(t):
-        here = pl.ds(t * step, step)
-        for k in range(1, rows):
-            back[t, k].wait_recv()
+    back, fold, grads = {}, {}, []
+
+    def send_fold(piece):
+        here = rows_of(piece)
+        for k in range(1, rows):
+            back[piece, k].wait_recv()
         for k in range(1, pairs):
 
             @pl.loop(0, wide)
             def _(b):
                 lanes = pl.ds(pl.multiple_of(b * blk, blk), blk)
-                value = gather_block(part_of(k) * wide + b, t)
+                value = gather_block(part_of(k) * wide + b, piece)
                 fold_out[k, here, lanes] = value.astype(jnp.bfloat16)
 
             copy = remote(
                 fold_out.at[k, here], fold_in.at[k, here],
-                fx_send.at[t, k], fx_recv.at[t, k], part_peer(k),
+                fx_send.at[piece, k], fx_recv.at[piece, k], part_peer(k),
             )
             copy.start()
-            fold[t, k] = copy
-
-    def sum_home(t):
-        @pl.loop(0, wide)
-        def _(b):
-            lanes = pl.ds(pl.multiple_of(b * blk, blk), blk)
-            home_sum[pl.ds(t * step, step), lanes] = gather_block(part * wide + b, t)
-
-    for t in range(chunks):
+            fold[piece, k] = copy
+
+    def forward(t):
         here = pl.ds(t * step, step)
-        for a in range(2):
-            for k in range(1, rows):
-                sel[a, t, k].wait_recv()
+        for k in range(1, rows):
+            sel[0, t, k].wait_recv()
 
         @each(total)
         def _(i):
-            block_out[i, here] = dot(x_sel[i, here], up_mat[i], 1, 0)
+            block_out[i] = dot(x_sel[i, here], up_mat[i], 1, 0)
+
+        @each(total)
+        def _(i):
+            spot, other = up_col(i), down_row(i)
+            hidden = jnp.zeros((step, blk), jnp.float32)
+            taken = jnp.zeros((step, blk), jnp.float32)
+            for j in range(total):
+                block = block_out[j]
+                hidden += flag((up_col(j) == spot) & (spot >= 0)) * block
+                taken += flag((up_col(j) == other) & (other >= 0)) * block
+            slope_at[i, here] = gelu_parts(hidden)[1]
+            act[i, here] = gelu_parts(taken)[0].astype(jnp.bfloat16)
+
+    def backward(t):
+        here = pl.ds(t * step, step)
+        for k in range(1, rows):
+            sel[1, t, k].wait_recv()
+
+        @each(total)
+        def _(i):
             down_part[i] = dot(y_sel[i, here], dn_mat[i], 1, 1)
 
         @each(total)
         def _(i):
             spot = up_col(i)
-            hidden = jnp.zeros((step, blk), jnp.float32)
             grad = jnp.zeros((step, blk), jnp.float32)
             for j in range(total):
-                hidden += flag((up_col(j) == spot) & (spot >= 0)) * block_out[j, here]
                 grad += flag((down_row(j) == spot) & (spot >= 0)) * down_part[j]
-            _, slope = gelu_parts(hidden)
-            dh = (grad * slope).astype(jnp.bfloat16)
+            dh = (grad * slope_at[i, here]).astype(jnp.bfloat16)
             dhid[i, here] = dh
             back_out[i, here] = dot(dh, up_mat[i], 1, 1).astype(jnp.bfloat16)
 
-        for k in range(1, rows):
-            copy = remote(
-                back_out.at[pl.ds(grp_of(k) * slots, slots), here],
-                back_in.at[pl.ds(group * slots, slots), here],
-                bk_send.at[t, k], bk_recv.at[t, k], grp_peer(k),
-            )
-            copy.start()
-            back[t, k] = copy
+        for piece in range(t * pieces, (t + 1) * pieces):
+            for k in range(1, rows):
+                copy = remote(
+                    back_out.at[pl.ds(grp_of(k) * slots, slots), rows_of(piece)],
+                    back_in.at[pl.ds(group * slots, slots), rows_of(piece)],
+                    bk_send.at[piece, k], bk_recv.at[piece, k], grp_peer(k),
+                )
+                copy.start()
+                back[piece, k] = copy
         for s in range(slots):
             back_in[group * slots + s, here] = back_out[group * slots + s, here]
-        if t > 0:
-            send_fold(t - 1)
-
-    @each(total)
-    def _(i):
-        spot = down_row(i)
-        hidden = jnp.zeros((tok, blk), jnp.float32)
-        for j in range(total):
-            hidden += flag((up_col(j) == spot) & (spot >= 0)) * block_out[j]
-        value, _ = gelu_parts(hidden)
-        act = value.astype(jnp.bfloat16)
-        term = dot(act, y_sel[i], 0, 0) * flag(spot >= 0)
-        dn_out[i] = term.astype(jnp.bfloat16)
-        term = dot(x_sel[i], dhid[i], 0, 0) * flag(up_col(i) >= 0)
-        up_out[i] = term.astype(jnp.bfloat16)
-
-    grads = []
-    for a, (src, dst) in enumerate(((up_out, up_in), (dn_out, dn_in))):
+
+    def send_grads(a, src, dst):
         for k in range(1, rows):
             copy = remote(
                 src.at[pl.ds(lax.rem(row + k, rows) * slots, slots)], dst.at[k],
@@ -346,15 +347,46 @@
             copy.start()
             grads.append(copy)
 
-    send_fold(chunks - 1)
+    for t in range(chunks - 1):
+        pick_send(t, 0)
+        pick_send(t, 1)
+    pick_send(chunks - 1, 0)
+    wait_mats()
+    forward(0)
+    pick_send(chunks - 1, 1)
     for t in range(chunks):
-        sum_home(t)
-
-    for t in range(chunks):
-        here = pl.ds(t * step, step)
+        if t > 0:
+            forward(t)
+        backward(t)
+
+    @each(total)
+    def _(i):
+        term = dot(act[i], y_sel[i], 0, 0) * flag(down_row(i) >= 0)
+        dn_out[i] = term.astype(jnp.bfloat16)
+
+    send_grads(1, dn_out, dn_in)
+
+    @each(total)
+    def _(i):
+        term = dot(x_sel[i], dhid[i], 0, 0) * flag(up_col(i) >= 0)
+        up_out[i] = term.astype(jnp.bfloat16)
+
+    send_grads(0, up_out, up_in)
+
+    for piece in range(chunks * pieces):
+        send_fold(piece)
+    for piece in range(chunks * pieces):
+
+        @pl.loop(0, wide)
+        def _(b):
+            lanes = pl.ds(pl.multiple_of(b * blk, blk), blk)
+            home_sum[rows_of(piece), lanes] = gather_block(part * wide + b, piece)
+
+    for piece in range(chunks * pieces):
+        here = rows_of(piece)
         value = home_sum[here]
         for k in range(1, pairs):
-            fold[t, k].wait_recv()
+            fold[piece, k].wait_recv()
             value += fold_in[k, here].astype(jnp.float32)
         gin_ref[here] = value.astype(jnp.bfloat16)
 
@@ -386,7 +418,7 @@
     slots, blk = up_blocks.shape[:2]
     tok, width = inputs.shape
     total = rows * slots
-    chunks = CHUNKS
+    chunks, pieces = CHUNKS, PIECES
     bf, f32 = jnp.bfloat16, jnp.float32
     dma = pltpu.SemaphoreType.DMA
     vmem, smem = pltpu.VMEM, pltpu.SMEM
@@ -407,9 +439,11 @@
         vmem((total, tok, blk), bf),
         vmem((total, blk, blk), bf),
         vmem((total, blk, blk), bf),
+        vmem((total, step, blk), f32),
+        vmem((total, step, blk), f32),
         vmem((total, tok, blk), f32),
-        vmem((total, step, blk), f32),
         vmem((tok, width), f32),
+        vmem((total, tok, blk), bf),
         vmem((total, tok, blk), bf),
         vmem((total, tok, blk), bf),
         vmem((total, tok, blk), bf),
@@ -425,13 +459,13 @@
     ]
     for shape in (
         (rows,), (rows,), (2, chunks, pairs), (2, rows),
-        (2, chunks, rows), (chunks, rows), (chunks, pairs), (2, rows),
+        (2, chunks, rows), (chunks * pieces, rows), (chunks * pieces, pairs), (2, rows),
     ):
         scratch += [dma(shape), dma(shape)]
     hbm = pl.BlockSpec(memory_space=pl.ANY)
     full = pl.BlockSpec(memory_space=pltpu.VMEM)
     return pl.pallas_call(
-        functools.partial(kernel, rows, pairs, slots, chunks),
+        functools.partial(kernel, rows, pairs, slots, chunks, pieces),
         out_shape=(
             vmem(inputs.shape, bf),
             vmem(up_blocks.shape, bf),

time: 38.7 us -> 38.4 us (level)
  no operation moved by 1% of the time
where the time goes in v6:
time: 38.4 us; the launch traced here: 38.2 us
  Pallas kernels  35.6 us (93%)
  local copies, waits for them, and re-layouts  1.96 us (5%)
  between operations  0.64 us (2%)
    pallas_call x1, Pallas kernels, body(): pl.pallas_call(functools.partial(kernel, rows, pairs, slots, chunks, piec...  35.6 us
    unnamed x3, local copies, waits for them, and re-layouts  1.96 us

profile of v6, /device:TPU:0, one launch (start us, length us, event | category | flops | bytes accessed | tf_op | source)
XLA Modules:
  0.0 38.2 jit_solution(13182808018355749786)
XLA Ops:
  0.6 35.6 %shard_map.85 = (bf16[128,1024]{1,0:T(8,128)(2,1)S(1)}, bf16[2,128,128]{2,1,0:T(8,128)(2,1)S(1)}, bf16[2,128,128]{2,1,0:T(8,128)(2,1)S(1)}) custom-call(bf16[128,1024]{1,0:T(8,128)(2,1)} %x_hbm.1, bf16[128,1024]{1,0:T(8,128)(2,1)} %y_hbm.1, bf16[2,128,128]{2,1,0:T(8,128)(2,1)} %up_hbm.1, bf16[2,128,128]{2,1,0:T(8,128)(2,1)} %dn_hbm.1, s32[2,2]{1,0:T(2,128)} %up_hpos.1, ...), custom_call_target="tpu_custom_call" | custom-call | tf_op jit(solution)/shard_map/pallas_call | solution.py:467
  36.2 0.7 %copy.12 = bf16[128,1024]{1,0:T(8,128)(2,1)} copy(bf16[128,1024]{1,0:T(8,128)(2,1)S(1)} %get-tuple-element.3) | data formatting | bytes 524288
  36.9 0.6 %copy.13 = bf16[2,128,128]{2,1,0:T(8,128)(2,1)} copy(bf16[2,128,128]{2,1,0:T(8,128)(2,1)S(1)} %get-tuple-element.4) | data formatting | bytes 131072
  37.6 0.6 %copy.14 = bf16[2,128,128]{2,1,0:T(8,128)(2,1)} copy(bf16[2,128,128]{2,1,0:T(8,128)(2,1)S(1)} %get-tuple-element.5) | data formatting | bytes 131072
